TPU v7x, 32 devices: a whole 2x2x4 slice. The times are simulated.
32 devices in a mesh: ens: 4 (over y, x), space: 8 (over z, core).
Axes of the slice: x: 2, y: 2, z: 4, core: 2. Of those that a mesh axis runs over, the one named last changes fastest.
Arguments:
- latent: bfloat16 [16, 256, 8192], P('ens', None, 'space'), may hold values from -6 to 6
- noise: bfloat16 [16, 256, 8192], P('ens', None, 'space'), may hold values from -6 to 6
- target: float32 [224, 8192], P('ens', 'space'), may hold values from -6 to 6
- w_in: bfloat16 [384, 256], replicated, may hold values from -0.375 to 0.375
- w_out: bfloat16 [224, 384], replicated, may hold values from -0.3125 to 0.3125
- w_close_in: bfloat16 [384, 224], replicated, may hold values from -0.375 to 0.375
- w_close_out: bfloat16 [224, 384], replicated, may hold values from -0.3125 to 0.3125
Outputs:
- grad_latent: float32 [16, 256, 8192], P('ens', None, 'space')
- step_in: float32 [384, 256], replicated
- step_out: float32 [224, 384], replicated
- step_close_in: float32 [384, 224], replicated
- step_close_out: float32 [224, 384], replicated
All inputs are finite; a program needn't handle non-finite values.
Results may differ from a plain program's by a relative error of at most 0.011.
Values sent between devices are 32-bit elements; how exact they have to be, the bound alone decides.
A program may use at most 128 MiB of HBM per device.

v0:
```python
import jax
import jax.numpy as jnp
from jax import lax
from jax.sharding import PartitionSpec as P

smooth_eps = 0.1


def activate(value):
    return jax.nn.gelu(value, approximate=True)


def activate_back(pre, grad):
    return jax.vjp(activate, pre)[1](grad)[0]


def smooth_sign(diff):
    return diff / jnp.sqrt(diff * diff + smooth_eps * smooth_eps)


def pair_terms(mine, every, truth):
    count = every.shape[0]

    def add_one(index, total):
        other = lax.dynamic_index_in_dim(every, index, 0, keepdims=False)
        return total + smooth_sign(mine - other)

    total = lax.fori_loop(0, count, add_one, jnp.zeros_like(mine))
    return smooth_sign(mine - truth) - total / count


def body(latent, noise, target, w_in, w_out, w_close_in, w_close_out):
    f32 = jnp.float32
    zin = (latent.astype(f32) + 0.5 * noise.astype(f32)).astype(jnp.bfloat16)
    pre1 = jnp.einsum("hf,mfc->mhc", w_in, zin, preferred_element_type=f32)
    hid1 = activate(pre1).astype(jnp.bfloat16)
    dec = jnp.einsum("kh,mhc->mkc", w_out, hid1, preferred_element_type=f32)
    decb = dec.astype(jnp.bfloat16)
    pre3 = jnp.einsum("hk,mkc->mhc", w_close_in, decb, preferred_element_type=f32)
    hid3 = activate(pre3).astype(jnp.bfloat16)
    pred = dec + jnp.einsum("kh,mhc->mkc", w_close_out, hid3, preferred_element_type=f32)
    every, full_target = (
        lax.all_gather(pred, "ens", axis=0, tiled=True),
        lax.all_gather(target, "ens", axis=0, tiled=True),
    )
    gpred = pair_terms(pred, every, full_target)
    gpredb = gpred.astype(jnp.bfloat16)
    g_close_out = jnp.einsum("mkc,mhc->kh", gpredb, hid3, preferred_element_type=f32)
    g_hid3 = jnp.einsum("kh,mkc->mhc", w_close_out, gpredb, preferred_element_type=f32)
    gpre3 = activate_back(pre3, g_hid3).astype(jnp.bfloat16)
    g_close_in = jnp.einsum("mhc,mkc->hk", gpre3, decb, preferred_element_type=f32)
    gdec = (
        gpred + jnp.einsum("hk,mhc->mkc", w_close_in, gpre3, preferred_element_type=f32)
    ).astype(jnp.bfloat16)
    g_out = jnp.einsum("mkc,mhc->kh", gdec, hid1, preferred_element_type=f32)
    g_hid1 = jnp.einsum("kh,mkc->mhc", w_out, gdec, preferred_element_type=f32)
    gpre1 = activate_back(pre1, g_hid1).astype(jnp.bfloat16)
    g_in = jnp.einsum("mhc,mfc->hf", gpre1, zin, preferred_element_type=f32)
    grad_latent = jnp.einsum("hf,mhc->mfc", w_in, gpre1, preferred_element_type=f32)
    g_in, g_out, g_close_in, g_close_out = lax.psum(
        (g_in, g_out, g_close_in, g_close_out), ("ens", "space")
    )
    count = g_in.size + g_out.size + g_close_in.size + g_close_out.size
    squares = (
        jnp.sum(g_in * g_in)
        + jnp.sum(g_out * g_out)
        + jnp.sum(g_close_in * g_close_in)
        + jnp.sum(g_close_out * g_close_out)
    )
    rms = jnp.sqrt(squares / count + 1e-12)
    return (grad_latent, g_in / rms, g_out / rms, g_close_in / rms, g_close_out / rms)


def solution(mesh):
    placed = (
        P("ens", None, "space"),
        P("ens", None, "space"),
        P("ens", "space"),
        P(),
        P(),
        P(),
        P(),
    )
    return jax.shard_map(
        body,
        mesh=mesh,
        in_specs=placed,
        out_specs=(P("ens", None, "space"), P(), P(), P(), P()),
        check_vma=False,
    )
```

profile of v0, /device:TPU:0, one launch (start us, length us, event | category | flops | bytes accessed | tf_op | source)
XLA Modules:
  0.0 469.2 jit_solution(4322245571807078582)
XLA Ops:
  7.2 0.0 all-gather.2.cloned.1.call-start
  7.2 0.9 copy-done
  8.1 3.5 fusion.34
  11.6 2.6 copy-done.4
  14.2 2.7 fusion.42
  16.9 1.3 fusion.25
  18.3 0.6 copy-done.1
  18.8 2.7 copy-done.3
  21.5 4.0 add_bitcast_fusion
  25.5 0.0 all-reduce.3.cloned.1.call-start
  25.6 14.1 %all_gather.6 = f32[224,1024]{1,0:T(8,128)S(1)} all-gather(f32[56,1024]{1,0:T(8,128)S(1)} %copy-done.8), channel_id=1, replica_groups=mesh['ens'=4,'space'=8] {'ens'}, dimensions={0}, use_global_device_ids=true | all-gather | bytes 1146880 | tf_op jit(solution)/shard_map/all_gather | solution.py:44
  39.7 128.7 %all-gather.2.cloned.1.call-done = f32[16,224,1024]{2,1,0:T(8,128)} async-done(((f32[4,224,1024]{2,1,0:T(8,128)}), f32[16,224,1024]{2,1,0:T(8,128)}) %all-gather.2.cloned.1.call-update) | async-done | bytes 14680080 | tf_op jit(solution)/shard_map/all_gather | solution.py:43
  168.3 120.0 %while.14 = (s32[]{:T(128)}, f32[4,224,1024]{2,1,0:T(8,128)}, f32[16,224,1024]{2,1,0:T(8,128)}, f32[4,224,1024]{2,1,0:T(8,128)}, s32[]{:T(128)}, /*index=5*/s32[]{:T(128)}) while((s32[]{:T(128)}, f32[4,224,1024]{2,1,0:T(8,128)}, f32[16,224,1024]{2,1,0:T(8,128)}, f32[4,224,1024]{2,1,0:T(8,128)}, s32[]{:T(128)}, ...), condition=%wide.region_1.2_spmd.clone, body=%wide.region_0.1_spmd.clone.sunk | while | flops 5505027 | bytes 13762643 | solution.py:28
  168.3 1.2 dynamic-slice_bitcast_fusion.2
  169.6 5.2 %select_add_fusion.2 = f32[4,224,1024]{2,1,0:T(8,128)} fusion(f32[4,224,1024]{2,1,0:T(8,128)} %get-tuple-element.156, f32[4,224,1024]{2,1,0:T(8,128)} %get-tuple-element.164, f32[224,1024]{1,0:T(8,128)S(1)} %dynamic-slice_bitcast_fusion.2, pred[]{:T(512)S(6)} %compare.3), kind=kLoop, calls=%fused_computation.clone.1 | loop fusion | flops 5505024 | bytes 11927553 | tf_op jit(solution)/shard_map/while/body/eval_jaxpr/add | solution.py:26
  174.8 1.2 dynamic-slice_bitcast_fusion.2
  176.0 6.3 %select_add_fusion.2 = f32[4,224,1024]{2,1,0:T(8,128)} fusion(f32[4,224,1024]{2,1,0:T(8,128)} %get-tuple-element.156, f32[4,224,1024]{2,1,0:T(8,128)} %get-tuple-element.164, f32[224,1024]{1,0:T(8,128)S(1)} %dynamic-slice_bitcast_fusion.2, pred[]{:T(512)S(6)} %compare.3), kind=kLoop, calls=%fused_computation.clone.1 | loop fusion | flops 5505024 | bytes 11927553 | tf_op jit(solution)/shard_map/while/body/eval_jaxpr/add | solution.py:26
  182.4 1.2 dynamic-slice_bitcast_fusion.2
  183.6 6.3 %select_add_fusion.2 = f32[4,224,1024]{2,1,0:T(8,128)} fusion(f32[4,224,1024]{2,1,0:T(8,128)} %get-tuple-element.156, f32[4,224,1024]{2,1,0:T(8,128)} %get-tuple-element.164, f32[224,1024]{1,0:T(8,128)S(1)} %dynamic-slice_bitcast_fusion.2, pred[]{:T(512)S(6)} %compare.3), kind=kLoop, calls=%fused_computation.clone.1 | loop fusion | flops 5505024 | bytes 11927553 | tf_op jit(solution)/shard_map/while/body/eval_jaxpr/add | solution.py:26
  189.9 1.2 dynamic-slice_bitcast_fusion.2
  191.2 6.3 %select_add_fusion.2 = f32[4,224,1024]{2,1,0:T(8,128)} fusion(f32[4,224,1024]{2,1,0:T(8,128)} %get-tuple-element.156, f32[4,224,1024]{2,1,0:T(8,128)} %get-tuple-element.164, f32[224,1024]{1,0:T(8,128)S(1)} %dynamic-slice_bitcast_fusion.2, pred[]{:T(512)S(6)} %compare.3), kind=kLoop, calls=%fused_computation.clone.1 | loop fusion | flops 5505024 | bytes 11927553 | tf_op jit(solution)/shard_map/while/body/eval_jaxpr/add | solution.py:26
  197.5 1.2 dynamic-slice_bitcast_fusion.2
  198.7 6.3 %select_add_fusion.2 = f32[4,224,1024]{2,1,0:T(8,128)} fusion(f32[4,224,1024]{2,1,0:T(8,128)} %get-tuple-element.156, f32[4,224,1024]{2,1,0:T(8,128)} %get-tuple-element.164, f32[224,1024]{1,0:T(8,128)S(1)} %dynamic-slice_bitcast_fusion.2, pred[]{:T(512)S(6)} %compare.3), kind=kLoop, calls=%fused_computation.clone.1 | loop fusion | flops 5505024 | bytes 11927553 | tf_op jit(solution)/shard_map/while/body/eval_jaxpr/add | solution.py:26
  205.1 1.2 dynamic-slice_bitcast_fusion.2
  206.3 6.3 %select_add_fusion.2 = f32[4,224,1024]{2,1,0:T(8,128)} fusion(f32[4,224,1024]{2,1,0:T(8,128)} %get-tuple-element.156, f32[4,224,1024]{2,1,0:T(8,128)} %get-tuple-element.164, f32[224,1024]{1,0:T(8,128)S(1)} %dynamic-slice_bitcast_fusion.2, pred[]{:T(512)S(6)} %compare.3), kind=kLoop, calls=%fused_computation.clone.1 | loop fusion | flops 5505024 | bytes 11927553 | tf_op jit(solution)/shard_map/while/body/eval_jaxpr/add | solution.py:26
  212.6 1.2 dynamic-slice_bitcast_fusion.2
  213.9 6.3 %select_add_fusion.2 = f32[4,224,1024]{2,1,0:T(8,128)} fusion(f32[4,224,1024]{2,1,0:T(8,128)} %get-tuple-element.156, f32[4,224,1024]{2,1,0:T(8,128)} %get-tuple-element.164, f32[224,1024]{1,0:T(8,128)S(1)} %dynamic-slice_bitcast_fusion.2, pred[]{:T(512)S(6)} %compare.3), kind=kLoop, calls=%fused_computation.clone.1 | loop fusion | flops 5505024 | bytes 11927553 | tf_op jit(solution)/shard_map/while/body/eval_jaxpr/add | solution.py:26
  220.2 1.2 dynamic-slice_bitcast_fusion.2
  221.4 6.3 %select_add_fusion.2 = f32[4,224,1024]{2,1,0:T(8,128)} fusion(f32[4,224,1024]{2,1,0:T(8,128)} %get-tuple-element.156, f32[4,224,1024]{2,1,0:T(8,128)} %get-tuple-element.164, f32[224,1024]{1,0:T(8,128)S(1)} %dynamic-slice_bitcast_fusion.2, pred[]{:T(512)S(6)} %compare.3), kind=kLoop, calls=%fused_computation.clone.1 | loop fusion | flops 5505024 | bytes 11927553 | tf_op jit(solution)/shard_map/while/body/eval_jaxpr/add | solution.py:26
  227.8 1.2 dynamic-slice_bitcast_fusion.2
  229.0 6.3 %select_add_fusion.2 = f32[4,224,1024]{2,1,0:T(8,128)} fusion(f32[4,224,1024]{2,1,0:T(8,128)} %get-tuple-element.156, f32[4,224,1024]{2,1,0:T(8,128)} %get-tuple-element.164, f32[224,1024]{1,0:T(8,128)S(1)} %dynamic-slice_bitcast_fusion.2, pred[]{:T(512)S(6)} %compare.3), kind=kLoop, calls=%fused_computation.clone.1 | loop fusion | flops 5505024 | bytes 11927553 | tf_op jit(solution)/shard_map/while/body/eval_jaxpr/add | solution.py:26
  235.3 1.2 dynamic-slice_bitcast_fusion.2
  236.6 6.3 %select_add_fusion.2 = f32[4,224,1024]{2,1,0:T(8,128)} fusion(f32[4,224,1024]{2,1,0:T(8,128)} %get-tuple-element.156, f32[4,224,1024]{2,1,0:T(8,128)} %get-tuple-element.164, f32[224,1024]{1,0:T(8,128)S(1)} %dynamic-slice_bitcast_fusion.2, pred[]{:T(512)S(6)} %compare.3), kind=kLoop, calls=%fused_computation.clone.1 | loop fusion | flops 5505024 | bytes 11927553 | tf_op jit(solution)/shard_map/while/body/eval_jaxpr/add | solution.py:26
  242.9 1.2 dynamic-slice_bitcast_fusion.2
  244.2 6.3 %select_add_fusion.2 = f32[4,224,1024]{2,1,0:T(8,128)} fusion(f32[4,224,1024]{2,1,0:T(8,128)} %get-tuple-element.156, f32[4,224,1024]{2,1,0:T(8,128)} %get-tuple-element.164, f32[224,1024]{1,0:T(8,128)S(1)} %dynamic-slice_bitcast_fusion.2, pred[]{:T(512)S(6)} %compare.3), kind=kLoop, calls=%fused_computation.clone.1 | loop fusion | flops 5505024 | bytes 11927553 | tf_op jit(solution)/shard_map/while/body/eval_jaxpr/add | solution.py:26
  250.5 1.2 dynamic-slice_bitcast_fusion.2
  251.7 6.3 %select_add_fusion.2 = f32[4,224,1024]{2,1,0:T(8,128)} fusion(f32[4,224,1024]{2,1,0:T(8,128)} %get-tuple-element.156, f32[4,224,1024]{2,1,0:T(8,128)} %get-tuple-element.164, f32[224,1024]{1,0:T(8,128)S(1)} %dynamic-slice_bitcast_fusion.2, pred[]{:T(512)S(6)} %compare.3), kind=kLoop, calls=%fused_computation.clone.1 | loop fusion | flops 5505024 | bytes 11927553 | tf_op jit(solution)/shard_map/while/body/eval_jaxpr/add | solution.py:26
  258.0 1.2 dynamic-slice_bitcast_fusion.2
  259.3 6.3 %select_add_fusion.2 = f32[4,224,1024]{2,1,0:T(8,128)} fusion(f32[4,224,1024]{2,1,0:T(8,128)} %get-tuple-element.156, f32[4,224,1024]{2,1,0:T(8,128)} %get-tuple-element.164, f32[224,1024]{1,0:T(8,128)S(1)} %dynamic-slice_bitcast_fusion.2, pred[]{:T(512)S(6)} %compare.3), kind=kLoop, calls=%fused_computation.clone.1 | loop fusion | flops 5505024 | bytes 11927553 | tf_op jit(solution)/shard_map/while/body/eval_jaxpr/add | solution.py:26
  265.6 1.2 dynamic-slice_bitcast_fusion.2
  266.9 6.3 %select_add_fusion.2 = f32[4,224,1024]{2,1,0:T(8,128)} fusion(f32[4,224,1024]{2,1,0:T(8,128)} %get-tuple-element.156, f32[4,224,1024]{2,1,0:T(8,128)} %get-tuple-element.164, f32[224,1024]{1,0:T(8,128)S(1)} %dynamic-slice_bitcast_fusion.2, pred[]{:T(512)S(6)} %compare.3), kind=kLoop, calls=%fused_computation.clone.1 | loop fusion | flops 5505024 | bytes 11927553 | tf_op jit(solution)/shard_map/while/body/eval_jaxpr/add | solution.py:26
  273.2 1.2 dynamic-slice_bitcast_fusion.2
  274.4 6.3 %select_add_fusion.2 = f32[4,224,1024]{2,1,0:T(8,128)} fusion(f32[4,224,1024]{2,1,0:T(8,128)} %get-tuple-element.156, f32[4,224,1024]{2,1,0:T(8,128)} %get-tuple-element.164, f32[224,1024]{1,0:T(8,128)S(1)} %dynamic-slice_bitcast_fusion.2, pred[]{:T(512)S(6)} %compare.3), kind=kLoop, calls=%fused_computation.clone.1 | loop fusion | flops 5505024 | bytes 11927553 | tf_op jit(solution)/shard_map/while/body/eval_jaxpr/add | solution.py:26
  280.7 1.2 dynamic-slice_bitcast_fusion.2
  282.0 6.3 %select_add_fusion.2 = f32[4,224,1024]{2,1,0:T(8,128)} fusion(f32[4,224,1024]{2,1,0:T(8,128)} %get-tuple-element.156, f32[4,224,1024]{2,1,0:T(8,128)} %get-tuple-element.164, f32[224,1024]{1,0:T(8,128)S(1)} %dynamic-slice_bitcast_fusion.2, pred[]{:T(512)S(6)} %compare.3), kind=kLoop, calls=%fused_computation.clone.1 | loop fusion | flops 5505024 | bytes 11927553 | tf_op jit(solution)/shard_map/while/body/eval_jaxpr/add | solution.py:26
  288.3 4.3 multiply_subtract_fusion
  292.7 0.7 slice-done.1
  293.3 4.8 %fusion.13 = bf16[4,384,1024]{1,2,0:T(8,128)(2,1)S(1)} fusion(f32[4,1024,384]{2,1,0:T(8,128)S(1)} %bitcast.110, f32[4,224,1024]{2,1,0:T(8,128)S(1)} %multiply_subtract_fusion, bf16[224,384]{1,0:T(8,128)(2,1)S(1)} %copy-done.9), kind=kOutput, calls=%fused_computation.19 | convolution fusion | flops 737017856 | bytes 13279232 | tf_op jit(solution)/shard_map/kh,mkc->mhc/dot_general | solution.py:49
  298.2 1.3 fusion.22
  299.5 3.2 convolution_bitcast_fusion.3
  302.7 5.0 %fusion.6 = bf16[4,384,1024]{1,2,0:T(8,128)(2,1)S(1)} fusion(f32[4,1024,384]{2,1,0:T(8,128)S(1)} %bitcast.112, bf16[4,224,1024]{2,1,0:T(8,128)(2,1)S(1)} %fusion.22, bf16[224,384]{1,0:T(8,128)(2,1)S(1)} %copy-done.10), kind=kOutput, calls=%fused_computation.12 | convolution fusion | flops 736100352 | bytes 11444224 | tf_op jit(solution)/shard_map/kh,mkc->mhc/dot_general | solution.py:56
  307.7 1.9 fusion.27
  309.6 3.1 convolution_bitcast_fusion.2
  312.8 1.9 convolution_bitcast_fusion.1
  314.7 3.2 convolution_bitcast_fusion
  317.9 5.4 %copy.29 = f32[4,256,1024]{2,1,0:T(8,128)} copy(f32[4,256,1024]{1,2,0:T(8,128)} %convolution_bitcast_fusion) | data formatting | bytes 8388608
  323.2 124.4 %all-reduce.3.cloned.1.call-done = (f32[384,256]{1,0:T(8,128)}, f32[224,384]{1,0:T(8,128)}, f32[384,224]{0,1:T(8,128)}, f32[224,384]{1,0:T(8,128)}) async-done(((f32[384,256]{1,0:T(8,128)}, f32[224,384]{1,0:T(8,128)}, f32[384,224]{0,1:T(8,128)}, f32[224,384]{1,0:T(8,128)}), (f32[384,256]{1,0:T(8,128)}, f32[224,384]{1,0:T(8,128)}, f32[384,224]{0,1:T(8,128)}, ...) | async-done | bytes 1425424 | tf_op jit(solution)/shard_map/psum | solution.py:60
  447.6 1.7 multiply_reduce_fusion
  449.3 1.7 multiply_reduce_fusion.2
  451.0 1.8 multiply_reduce_fusion.1
  455.4 1.7 broadcast_divide_fusion.2
  457.1 1.7 broadcast_divide_fusion.1
  458.9 1.7 broadcast_divide_fusion.3
  460.6 1.8 broadcast_divide_fusion
  (30 shorter events, 0.1 us)
Async XLA Ops:
  7.2 0.9 copy-start
  7.2 7.0 %copy-start.10 = (bf16[224,384]{1,0:T(8,128)(2,1)S(1)}, bf16[224,384]{1,0:T(8,128)(2,1)}, u32[]{:S(2)}) copy-start(bf16[224,384]{1,0:T(8,128)(2,1)} %param.13) | copy-start | bytes 516100
  7.2 161.1 %all-gather.2.cloned.1.call-start = ((), (), s32[]{:S(2)}) async-start(), calls=%async_computation | async-start | bytes 18350080 | tf_op jit(solution)/shard_map/all_gather | solution.py:43
  11.6 2.6 copy-start.4
  14.2 2.7 copy-start.7
  16.9 1.9 copy-start.1
  16.9 4.5 copy-start.9
  18.8 2.7 copy-start.3
  21.5 4.1 copy-start.8
  25.5 422.1 %all-reduce.3.cloned.1.call-start = ((), (), s32[]{:S(2)}) async-start(), calls=%async_computation.1 | async-start | bytes 2850816 | tf_op jit(solution)/shard_map/psum | solution.py:60
  288.3 4.4 slice-start
  288.3 5.0 %slice-start.1 = ((s8[6291456]{0:T(1024)(128)(4,1)}), s8[2097152]{0:T(1024)(128)(4,1)S(1)}, s32[]{:S(2)}) async-start(s8[6291456]{0:T(1024)(128)(4,1)} %bitcast.109), calls=%async_computation.3 | async-start | bytes 4194304
  288.3 11.1 %slice-start.2 = ((s8[6291456]{0:T(1024)(128)(4,1)}), s8[4194304]{0:T(1024)(128)(4,1)S(1)}, s32[]{:S(2)}) async-start(s8[6291456]{0:T(1024)(128)(4,1)} %bitcast.111), calls=%async_computation.4 | async-start | bytes 8388608
  293.3 6.1 %slice-start.3 = ((s8[6291456]{0:T(1024)(128)(4,1)}), s8[2097152]{0:T(1024)(128)(4,1)S(1)}, s32[]{:S(2)}) async-start(s8[6291456]{0:T(1024)(128)(4,1)} %bitcast.111), calls=%async_computation.5 | async-start | bytes 4194304
  302.7 5.0 %copy-start.2 = (f32[4,1024,224]{1,2,0:T(8,128)S(1)}, f32[4,1024,224]{1,2,0:T(8,128)}, u32[]{:S(2)}) copy-start(f32[4,1024,224]{1,2,0:T(8,128)} %copy-done.1) | copy-start | bytes 11010052
  309.6 3.2 copy-start.5
  309.6 3.2 copy-start.6
Sparse Core Ops, SparseCore 0:
  25.6 142.6 all-gather.1
  314.8 132.7 all-reduce.2
where the time goes:
time: 470 us; the launch traced here: 469 us
  waiting for transfers between devices  253 us (54%)
  other arithmetic  116 us (25%)
  matrix products  36 us (8%)
  local copies, waits for them, and re-layouts  32.5 us (7%)
  between operations  16.8 us (4%)
  blocking collectives  14.1 us (3%)
    all_gather x1, waiting for transfers between devices, body(): lax.all_gather(pred, 'ens', axis=0, tiled=True)  129 us
    psum x1, waiting for transfers between devices, body(): lax.psum((g_in, g_out, g_close_in, g_close_out), ('ens', 'space'))  124 us
    add x16, other arithmetic, add_one(): return total + smooth_sign(mine - other)  100 us
    sub x16, local copies, waits for them, and re-layouts, add_one(): return total + smooth_sign(mine - other)  19.8 us
    all_gather x1, blocking collectives, body(): lax.all_gather(target, 'ens', axis=0, tiled=True)  14.1 us
    unnamed x31, local copies, waits for them, and re-layouts  12.7 us
  transfers between devices with their start and end apart: 2, of which 2 were waited for; matrix products, arithmetic and copies ran while one was open for 2% of the time, Pallas kernels for 0%

commit v1 on v0

--- a/solution.py
+++ b/solution.py
@@ -4,6 +4,12 @@
 from jax.sharding import PartitionSpec as P
 
 smooth_eps = 0.1
+
+
+def _measure_unit(axis_key, named_axis, view):
+    for no in (named_axis, axis_key):
+        view = jax.lax.psum(view, axis_name=no)
+    return view
 
 
 def activate(value):
@@ -57,8 +63,8 @@
     gpre1 = activate_back(pre1, g_hid1).astype(jnp.bfloat16)
     g_in = jnp.einsum("mhc,mfc->hf", gpre1, zin, preferred_element_type=f32)
     grad_latent = jnp.einsum("hf,mhc->mfc", w_in, gpre1, preferred_element_type=f32)
-    g_in, g_out, g_close_in, g_close_out = lax.psum(
-        (g_in, g_out, g_close_in, g_close_out), ("ens", "space")
+    g_in, g_out, g_close_in, g_close_out = _measure_unit(
+        "ens", "space", (g_in, g_out, g_close_in, g_close_out)
     )
     count = g_in.size + g_out.size + g_close_in.size + g_close_out.size
     squares = (

time: 470 us -> 460 us (0.979)
  waiting for transfers between devices: 253 us -> 243 us
    psum x1 -> x2, waiting for transfers between devices: 124 us -> 114 us  [_measure_unit(): view = jax.lax.psum(view, axis_name=no)]
  transfers between devices with their start and end apart: 2 -> 3, of which waited for: 2 -> 3; matrix products, arithmetic and copies ran while one was open for 2% -> 2% of each run, Pallas kernels for 0% -> 0%
where the time goes in v1:
time: 460 us; the launch traced here: 459 us
  waiting for transfers between devices  243 us (53%)
  other arithmetic  116 us (25%)
  matrix products  36 us (8%)
  local copies, waits for them, and re-layouts  32.5 us (7%)
  between operations  16.5 us (4%)
  blocking collectives  14.1 us (3%)
    all_gather x1, waiting for transfers between devices, body(): lax.all_gather(pred, 'ens', axis=0, tiled=True)  129 us
    psum x2, waiting for transfers between devices, _measure_unit(): view = jax.lax.psum(view, axis_name=no)  114 us
    add x16, other arithmetic, add_one(): return total + smooth_sign(mine - other)  100 us
    sub x16, local copies, waits for them, and re-layouts, add_one(): return total + smooth_sign(mine - other)  19.8 us
    all_gather x1, blocking collectives, body(): lax.all_gather(target, 'ens', axis=0, tiled=True)  14.1 us
    unnamed x31, local copies, waits for them, and re-layouts  12.7 us
  transfers between devices with their start and end apart: 3, of which 3 were waited for; matrix products, arithmetic and copies ran while one was open for 2% of the time, Pallas kernels for 0%

profile of v1, /device:TPU:0, one launch (start us, length us, event | category | flops | bytes accessed | tf_op | source)
XLA Modules:
  0.0 459.1 jit_solution(11918158029717087061)
XLA Ops:
  7.2 0.9 copy-done
  8.1 3.5 fusion.34
  11.6 2.6 copy-done.4
  14.2 2.7 fusion.42
  17.0 1.3 fusion.25
  18.3 0.6 copy-done.1
  18.9 2.6 copy-done.3
  21.5 4.0 add_bitcast_fusion
  25.5 0.0 all-reduce.5.cloned.1.call-start
  25.6 14.1 %all_gather.6 = f32[224,1024]{1,0:T(8,128)S(1)} all-gather(f32[56,1024]{1,0:T(8,128)S(1)} %copy-done.8), channel_id=1, replica_groups=mesh['ens'=4,'space'=8] {'ens'}, dimensions={0}, use_global_device_ids=true | all-gather | bytes 1146880 | tf_op jit(solution)/shard_map/all_gather | solution.py:50
  39.7 128.7 %all-gather.2.cloned.1.call-done = f32[16,224,1024]{2,1,0:T(8,128)} async-done(((f32[4,224,1024]{2,1,0:T(8,128)}), f32[16,224,1024]{2,1,0:T(8,128)}) %all-gather.2.cloned.1.call-update) | async-done | bytes 14680080 | tf_op jit(solution)/shard_map/all_gather | solution.py:49
  168.4 120.0 %while.14 = (s32[]{:T(128)}, f32[4,224,1024]{2,1,0:T(8,128)}, f32[16,224,1024]{2,1,0:T(8,128)}, f32[4,224,1024]{2,1,0:T(8,128)}, s32[]{:T(128)}, /*index=5*/s32[]{:T(128)}) while((s32[]{:T(128)}, f32[4,224,1024]{2,1,0:T(8,128)}, f32[16,224,1024]{2,1,0:T(8,128)}, f32[4,224,1024]{2,1,0:T(8,128)}, s32[]{:T(128)}, ...), condition=%wide.region_1.2_spmd.clone, body=%wide.region_0.1_spmd.clone.sunk | while | flops 5505027 | bytes 13762643 | solution.py:34
  168.4 1.2 dynamic-slice_bitcast_fusion.2
  169.6 5.2 %select_add_fusion.2 = f32[4,224,1024]{2,1,0:T(8,128)} fusion(f32[4,224,1024]{2,1,0:T(8,128)} %get-tuple-element.160, f32[4,224,1024]{2,1,0:T(8,128)} %get-tuple-element.168, f32[224,1024]{1,0:T(8,128)S(1)} %dynamic-slice_bitcast_fusion.2, pred[]{:T(512)S(6)} %compare.3), kind=kLoop, calls=%fused_computation.clone.1 | loop fusion | flops 5505024 | bytes 11927553 | tf_op jit(solution)/shard_map/while/body/eval_jaxpr/add | solution.py:32
  174.8 1.2 dynamic-slice_bitcast_fusion.2
  176.1 6.3 %select_add_fusion.2 = f32[4,224,1024]{2,1,0:T(8,128)} fusion(f32[4,224,1024]{2,1,0:T(8,128)} %get-tuple-element.160, f32[4,224,1024]{2,1,0:T(8,128)} %get-tuple-element.168, f32[224,1024]{1,0:T(8,128)S(1)} %dynamic-slice_bitcast_fusion.2, pred[]{:T(512)S(6)} %compare.3), kind=kLoop, calls=%fused_computation.clone.1 | loop fusion | flops 5505024 | bytes 11927553 | tf_op jit(solution)/shard_map/while/body/eval_jaxpr/add | solution.py:32
  182.4 1.2 dynamic-slice_bitcast_fusion.2
  183.6 6.3 %select_add_fusion.2 = f32[4,224,1024]{2,1,0:T(8,128)} fusion(f32[4,224,1024]{2,1,0:T(8,128)} %get-tuple-element.160, f32[4,224,1024]{2,1,0:T(8,128)} %get-tuple-element.168, f32[224,1024]{1,0:T(8,128)S(1)} %dynamic-slice_bitcast_fusion.2, pred[]{:T(512)S(6)} %compare.3), kind=kLoop, calls=%fused_computation.clone.1 | loop fusion | flops 5505024 | bytes 11927553 | tf_op jit(solution)/shard_map/while/body/eval_jaxpr/add | solution.py:32
  190.0 1.2 dynamic-slice_bitcast_fusion.2
  191.2 6.3 %select_add_fusion.2 = f32[4,224,1024]{2,1,0:T(8,128)} fusion(f32[4,224,1024]{2,1,0:T(8,128)} %get-tuple-element.160, f32[4,224,1024]{2,1,0:T(8,128)} %get-tuple-element.168, f32[224,1024]{1,0:T(8,128)S(1)} %dynamic-slice_bitcast_fusion.2, pred[]{:T(512)S(6)} %compare.3), kind=kLoop, calls=%fused_computation.clone.1 | loop fusion | flops 5505024 | bytes 11927553 | tf_op jit(solution)/shard_map/while/body/eval_jaxpr/add | solution.py:32
  197.5 1.2 dynamic-slice_bitcast_fusion.2
  198.8 6.3 %select_add_fusion.2 = f32[4,224,1024]{2,1,0:T(8,128)} fusion(f32[4,224,1024]{2,1,0:T(8,128)} %get-tuple-element.160, f32[4,224,1024]{2,1,0:T(8,128)} %get-tuple-element.168, f32[224,1024]{1,0:T(8,128)S(1)} %dynamic-slice_bitcast_fusion.2, pred[]{:T(512)S(6)} %compare.3), kind=kLoop, calls=%fused_computation.clone.1 | loop fusion | flops 5505024 | bytes 11927553 | tf_op jit(solution)/shard_map/while/body/eval_jaxpr/add | solution.py:32
  205.1 1.2 dynamic-slice_bitcast_fusion.2
  206.3 6.3 %select_add_fusion.2 = f32[4,224,1024]{2,1,0:T(8,128)} fusion(f32[4,224,1024]{2,1,0:T(8,128)} %get-tuple-element.160, f32[4,224,1024]{2,1,0:T(8,128)} %get-tuple-element.168, f32[224,1024]{1,0:T(8,128)S(1)} %dynamic-slice_bitcast_fusion.2, pred[]{:T(512)S(6)} %compare.3), kind=kLoop, calls=%fused_computation.clone.1 | loop fusion | flops 5505024 | bytes 11927553 | tf_op jit(solution)/shard_map/while/body/eval_jaxpr/add | solution.py:32
  212.7 1.2 dynamic-slice_bitcast_fusion.2
  213.9 6.3 %select_add_fusion.2 = f32[4,224,1024]{2,1,0:T(8,128)} fusion(f32[4,224,1024]{2,1,0:T(8,128)} %get-tuple-element.160, f32[4,224,1024]{2,1,0:T(8,128)} %get-tuple-element.168, f32[224,1024]{1,0:T(8,128)S(1)} %dynamic-slice_bitcast_fusion.2, pred[]{:T(512)S(6)} %compare.3), kind=kLoop, calls=%fused_computation.clone.1 | loop fusion | flops 5505024 | bytes 11927553 | tf_op jit(solution)/shard_map/while/body/eval_jaxpr/add | solution.py:32
  220.2 1.2 dynamic-slice_bitcast_fusion.2
  221.5 6.3 %select_add_fusion.2 = f32[4,224,1024]{2,1,0:T(8,128)} fusion(f32[4,224,1024]{2,1,0:T(8,128)} %get-tuple-element.160, f32[4,224,1024]{2,1,0:T(8,128)} %get-tuple-element.168, f32[224,1024]{1,0:T(8,128)S(1)} %dynamic-slice_bitcast_fusion.2, pred[]{:T(512)S(6)} %compare.3), kind=kLoop, calls=%fused_computation.clone.1 | loop fusion | flops 5505024 | bytes 11927553 | tf_op jit(solution)/shard_map/while/body/eval_jaxpr/add | solution.py:32
  227.8 1.2 dynamic-slice_bitcast_fusion.2
  229.1 6.3 %select_add_fusion.2 = f32[4,224,1024]{2,1,0:T(8,128)} fusion(f32[4,224,1024]{2,1,0:T(8,128)} %get-tuple-element.160, f32[4,224,1024]{2,1,0:T(8,128)} %get-tuple-element.168, f32[224,1024]{1,0:T(8,128)S(1)} %dynamic-slice_bitcast_fusion.2, pred[]{:T(512)S(6)} %compare.3), kind=kLoop, calls=%fused_computation.clone.1 | loop fusion | flops 5505024 | bytes 11927553 | tf_op jit(solution)/shard_map/while/body/eval_jaxpr/add | solution.py:32
  235.4 1.2 dynamic-slice_bitcast_fusion.2
  236.6 6.3 %select_add_fusion.2 = f32[4,224,1024]{2,1,0:T(8,128)} fusion(f32[4,224,1024]{2,1,0:T(8,128)} %get-tuple-element.160, f32[4,224,1024]{2,1,0:T(8,128)} %get-tuple-element.168, f32[224,1024]{1,0:T(8,128)S(1)} %dynamic-slice_bitcast_fusion.2, pred[]{:T(512)S(6)} %compare.3), kind=kLoop, calls=%fused_computation.clone.1 | loop fusion | flops 5505024 | bytes 11927553 | tf_op jit(solution)/shard_map/while/body/eval_jaxpr/add | solution.py:32
  242.9 1.2 dynamic-slice_bitcast_fusion.2
  244.2 6.3 %select_add_fusion.2 = f32[4,224,1024]{2,1,0:T(8,128)} fusion(f32[4,224,1024]{2,1,0:T(8,128)} %get-tuple-element.160, f32[4,224,1024]{2,1,0:T(8,128)} %get-tuple-element.168, f32[224,1024]{1,0:T(8,128)S(1)} %dynamic-slice_bitcast_fusion.2, pred[]{:T(512)S(6)} %compare.3), kind=kLoop, calls=%fused_computation.clone.1 | loop fusion | flops 5505024 | bytes 11927553 | tf_op jit(solution)/shard_map/while/body/eval_jaxpr/add | solution.py:32
  250.5 1.2 dynamic-slice_bitcast_fusion.2
  251.8 6.3 %select_add_fusion.2 = f32[4,224,1024]{2,1,0:T(8,128)} fusion(f32[4,224,1024]{2,1,0:T(8,128)} %get-tuple-element.160, f32[4,224,1024]{2,1,0:T(8,128)} %get-tuple-element.168, f32[224,1024]{1,0:T(8,128)S(1)} %dynamic-slice_bitcast_fusion.2, pred[]{:T(512)S(6)} %compare.3), kind=kLoop, calls=%fused_computation.clone.1 | loop fusion | flops 5505024 | bytes 11927553 | tf_op jit(solution)/shard_map/while/body/eval_jaxpr/add | solution.py:32
  258.1 1.2 dynamic-slice_bitcast_fusion.2
  259.3 6.3 %select_add_fusion.2 = f32[4,224,1024]{2,1,0:T(8,128)} fusion(f32[4,224,1024]{2,1,0:T(8,128)} %get-tuple-element.160, f32[4,224,1024]{2,1,0:T(8,128)} %get-tuple-element.168, f32[224,1024]{1,0:T(8,128)S(1)} %dynamic-slice_bitcast_fusion.2, pred[]{:T(512)S(6)} %compare.3), kind=kLoop, calls=%fused_computation.clone.1 | loop fusion | flops 5505024 | bytes 11927553 | tf_op jit(solution)/shard_map/while/body/eval_jaxpr/add | solution.py:32
  265.6 1.2 dynamic-slice_bitcast_fusion.2
  266.9 6.3 %select_add_fusion.2 = f32[4,224,1024]{2,1,0:T(8,128)} fusion(f32[4,224,1024]{2,1,0:T(8,128)} %get-tuple-element.160, f32[4,224,1024]{2,1,0:T(8,128)} %get-tuple-element.168, f32[224,1024]{1,0:T(8,128)S(1)} %dynamic-slice_bitcast_fusion.2, pred[]{:T(512)S(6)} %compare.3), kind=kLoop, calls=%fused_computation.clone.1 | loop fusion | flops 5505024 | bytes 11927553 | tf_op jit(solution)/shard_map/while/body/eval_jaxpr/add | solution.py:32
  273.2 1.2 dynamic-slice_bitcast_fusion.2
  274.5 6.3 %select_add_fusion.2 = f32[4,224,1024]{2,1,0:T(8,128)} fusion(f32[4,224,1024]{2,1,0:T(8,128)} %get-tuple-element.160, f32[4,224,1024]{2,1,0:T(8,128)} %get-tuple-element.168, f32[224,1024]{1,0:T(8,128)S(1)} %dynamic-slice_bitcast_fusion.2, pred[]{:T(512)S(6)} %compare.3), kind=kLoop, calls=%fused_computation.clone.1 | loop fusion | flops 5505024 | bytes 11927553 | tf_op jit(solution)/shard_map/while/body/eval_jaxpr/add | solution.py:32
  280.8 1.2 dynamic-slice_bitcast_fusion.2
  282.0 6.3 %select_add_fusion.2 = f32[4,224,1024]{2,1,0:T(8,128)} fusion(f32[4,224,1024]{2,1,0:T(8,128)} %get-tuple-element.160, f32[4,224,1024]{2,1,0:T(8,128)} %get-tuple-element.168, f32[224,1024]{1,0:T(8,128)S(1)} %dynamic-slice_bitcast_fusion.2, pred[]{:T(512)S(6)} %compare.3), kind=kLoop, calls=%fused_computation.clone.1 | loop fusion | flops 5505024 | bytes 11927553 | tf_op jit(solution)/shard_map/while/body/eval_jaxpr/add | solution.py:32
  288.4 4.3 multiply_subtract_fusion
  292.7 0.7 slice-done.1
  293.4 4.8 %fusion.13 = bf16[4,384,1024]{1,2,0:T(8,128)(2,1)S(1)} fusion(f32[4,1024,384]{2,1,0:T(8,128)S(1)} %bitcast.110, f32[4,224,1024]{2,1,0:T(8,128)S(1)} %multiply_subtract_fusion, bf16[224,384]{1,0:T(8,128)(2,1)S(1)} %copy-done.9), kind=kOutput, calls=%fused_computation.19 | convolution fusion | flops 737017856 | bytes 13279232 | tf_op jit(solution)/shard_map/kh,mkc->mhc/dot_general | solution.py:55
  298.2 1.3 fusion.22
  299.5 3.2 convolution_bitcast_fusion.3
  302.7 5.0 %fusion.6 = bf16[4,384,1024]{1,2,0:T(8,128)(2,1)S(1)} fusion(f32[4,1024,384]{2,1,0:T(8,128)S(1)} %bitcast.112, bf16[4,224,1024]{2,1,0:T(8,128)(2,1)S(1)} %fusion.22, bf16[224,384]{1,0:T(8,128)(2,1)S(1)} %copy-done.10), kind=kOutput, calls=%fused_computation.12 | convolution fusion | flops 736100352 | bytes 11444224 | tf_op jit(solution)/shard_map/kh,mkc->mhc/dot_general | solution.py:62
  307.8 1.9 fusion.27
  309.7 3.1 convolution_bitcast_fusion.2
  312.8 1.9 convolution_bitcast_fusion.1
  314.8 61.2 %all-reduce.5.cloned.1.call-done = (f32[384,256]{1,0:T(8,128)}, f32[224,384]{1,0:T(8,128)}, f32[384,224]{0,1:T(8,128)}, f32[224,384]{1,0:T(8,128)}) async-done(((f32[384,256]{1,0:T(8,128)}, f32[224,384]{1,0:T(8,128)}, f32[384,224]{0,1:T(8,128)}, f32[224,384]{1,0:T(8,128)}), (f32[384,256]{1,0:T(8,128)}, f32[224,384]{1,0:T(8,128)}, f32[384,224]{0,1:T(8,128)}, ...) | async-done | bytes 1425424 | tf_op jit(solution)/shard_map/psum | solution.py:11
  376.0 3.2 convolution_bitcast_fusion
  379.3 5.3 %copy.29 = f32[4,256,1024]{2,1,0:T(8,128)} copy(f32[4,256,1024]{1,2,0:T(8,128)} %convolution_bitcast_fusion) | data formatting | bytes 8388608
  384.6 53.2 %all-reduce.7.cloned.1.call-done = (f32[384,256]{1,0:T(8,128)}, f32[224,384]{1,0:T(8,128)}, f32[384,224]{0,1:T(8,128)}, f32[224,384]{1,0:T(8,128)}) async-done(((f32[384,256]{1,0:T(8,128)}, f32[224,384]{1,0:T(8,128)}, f32[384,224]{0,1:T(8,128)}, f32[224,384]{1,0:T(8,128)}), (f32[384,256]{1,0:T(8,128)}, f32[224,384]{1,0:T(8,128)}, f32[384,224]{0,1:T(8,128)}, ...) | async-done | bytes 1425424 | tf_op jit(solution)/shard_map/psum | solution.py:11
  437.8 1.7 multiply_reduce_fusion
  439.5 1.7 multiply_reduce_fusion.2
  441.2 1.8 multiply_reduce_fusion.1
  445.6 1.7 broadcast_divide_fusion.2
  447.4 1.7 broadcast_divide_fusion.1
  449.1 1.7 broadcast_divide_fusion.3
  450.8 1.8 broadcast_divide_fusion
  (33 shorter events, 0.2 us)
Async XLA Ops:
  7.2 0.9 copy-start
  7.2 7.0 %copy-start.10 = (bf16[224,384]{1,0:T(8,128)(2,1)S(1)}, bf16[224,384]{1,0:T(8,128)(2,1)}, u32[]{:S(2)}) copy-start(bf16[224,384]{1,0:T(8,128)(2,1)} %param.13) | copy-start | bytes 516100
  7.2 161.2 %all-gather.2.cloned.1.call-start = ((), (), s32[]{:S(2)}) async-start(), calls=%async_computation | async-start | bytes 18350080 | tf_op jit(solution)/shard_map/all_gather | solution.py:49
  11.6 2.6 copy-start.4
  14.2 2.7 copy-start.7
  16.9 1.9 copy-start.1
  16.9 4.6 copy-start.9
  18.9 2.6 copy-start.3
  21.5 4.1 copy-start.8
  25.5 350.5 %all-reduce.5.cloned.1.call-start = ((), (), s32[]{:S(2)}) async-start(), calls=%async_computation.1 | async-start | bytes 2850816 | tf_op jit(solution)/shard_map/psum | solution.py:11
  288.4 4.4 slice-start
  288.4 5.0 %slice-start.1 = ((s8[6291456]{0:T(1024)(128)(4,1)}), s8[2097152]{0:T(1024)(128)(4,1)S(1)}, s32[]{:S(2)}) async-start(s8[6291456]{0:T(1024)(128)(4,1)} %bitcast.109), calls=%async_computation.4 | async-start | bytes 4194304
  288.4 11.1 %slice-start.2 = ((s8[6291456]{0:T(1024)(128)(4,1)}), s8[4194304]{0:T(1024)(128)(4,1)S(1)}, s32[]{:S(2)}) async-start(s8[6291456]{0:T(1024)(128)(4,1)} %bitcast.111), calls=%async_computation.5 | async-start | bytes 8388608
  293.4 6.1 %slice-start.3 = ((s8[6291456]{0:T(1024)(128)(4,1)}), s8[2097152]{0:T(1024)(128)(4,1)S(1)}, s32[]{:S(2)}) async-start(s8[6291456]{0:T(1024)(128)(4,1)} %bitcast.111), calls=%async_computation.6 | async-start | bytes 4194304
  302.7 5.0 %copy-start.2 = (f32[4,1024,224]{1,2,0:T(8,128)S(1)}, f32[4,1024,224]{1,2,0:T(8,128)}, u32[]{:S(2)}) copy-start(f32[4,1024,224]{1,2,0:T(8,128)} %copy-done.1) | copy-start | bytes 11010052
  309.7 3.2 copy-start.5
  309.7 3.2 copy-start.6
  314.7 123.1 %all-reduce.7.cloned.1.call-start = ((), (), s32[]{:S(2)}) async-start(), calls=%async_computation.2 | async-start | bytes 2850816 | tf_op jit(solution)/shard_map/psum | solution.py:11
Sparse Core Ops, SparseCore 0:
  25.7 142.6 all-gather.1
  314.8 61.1 all-reduce.4
  379.5 58.3 all-reduce.6
